TPU v7x, 128 devices: a whole 4x4x4 slice. The times are simulated.
128 devices in a mesh: row: 8 (over y, core), col: 16 (over z, x).
Axes of the slice: x: 4, y: 4, z: 4, core: 2. Of those that a mesh axis runs over, the one named last changes fastest.
Arguments:
- hidden_states: bfloat16 [1024, 2048], P('col', 'row'), may hold values from -20 to 20
- input_gain: float32 [2, 2048], P(None, 'row'), may hold values from 0.25 to 1.75
- inner_weight: bfloat16 [2, 2048, 2, 4096], P(None, 'row', None, 'col'), may hold values from -0.125 to 0.125
- proj_weight: bfloat16 [2, 2048, 256], P(None, 'row'), may hold values from -0.125 to 0.125
- step_weight: bfloat16 [2, 2048, 64], P(None, 'row', 'col'), may hold values from -0.125 to 0.125
- inner_kernel: float32 [2, 4, 4096], P(None, None, 'col'), may hold values from -3 to 3
- proj_kernel: float32 [2, 4, 256], replicated, may hold values from -3 to 3
- step_bias: float32 [2, 64], P(None, 'col'), may hold values from -5 to -1
- decay_log: float32 [2, 64], P(None, 'col'), may hold values from -2 to 1
- skip_gain: float32 [2, 64], P(None, 'col'), may hold values from 0.5 to 1.5
- norm_gain: float32 [2, 4096], P(None, 'col'), may hold values from 0.25 to 1.75
- out_weight: bfloat16 [2, 4096, 2048], P(None, 'col', 'row'), may hold values from -0.09375 to 0.09375
- inner_cache: bfloat16 [2, 64, 3, 4096], P(None, 'row', None, 'col'), may hold values from -6 to 6
- proj_cache: bfloat16 [2, 64, 3, 256], P(None, 'row'), may hold values from -6 to 6
- state_cache: float32 [2, 64, 64, 64, 128], P(None, 'row', 'col'), may hold values from -1.2 to 1.2
- accepted: int32 [64], P('row'), may hold values from 1 to 16
- owners: int32 [64], P('row'), may hold values from 0 to 15, as said below
- tenant_ranges: int32 [4, 2], replicated, may hold values from 0 to 64, as said below
Outputs:
- hidden_output: bfloat16 [1024, 2048], P('col', 'row')
- step_states: bfloat16 [2, 64, 16, 64, 64, 128], P(None, 'row', None, 'col')
- owned_states: bfloat16 [8, 16, 2, 2, 64, 64, 128], P('row', 'col')
Inputs may be any that keep to these rules, and one draw needn't show every extreme that they name: `owners`: within the requests of one index of row (aligned blocks of 8) no owner appears more than 2 times, and in every block some owner appears exactly 2 times. `tenant_ranges`: the ranges are in order, disjoint and not empty; exactly 8 requests lie in no range.
All inputs are finite; a program needn't handle non-finite values.
Results may differ from a plain program's by a relative error of at most 0.024.
Values may be sent and summed in bfloat16 or wider, within the bound.
No kernel may reach another device: no remote copies, remote signals or barrier semaphores. Data moves between devices by JAX's collectives and lax.ppermute only.
A program may use at most 128 MiB of HBM per device.

v0:
```python
import jax
import jax.numpy as jnp
from jax import lax
from jax.sharding import PartitionSpec as P

S = 16
SEND_CAP = 2
EPSILON = 1e-05


def conv_silu(prefix, incoming, kernel):
    joined = jnp.concatenate([prefix, incoming], axis=1)
    length = incoming.shape[1]
    summed = joined[:, 0:length, :] * kernel[0]
    for offset in range(1, kernel.shape[0]):
        summed = summed + joined[:, offset : offset + length, :] * kernel[offset]
    return jax.nn.silu(summed)


def ssm_scan(decays, deltas, inner_values, b_values, c_values, skip_values, start_state):

    def advance(carried, packed):
        decay_now, delta_now, value_now, b_now, c_now = packed
        updated = (
            decay_now[:, :, None, None] * carried
            + (delta_now[:, :, None] * value_now)[:, :, :, None] * b_now[:, None, None, :]
        )
        output = (
            jnp.einsum("rhpn,rn->rhp", updated, c_now, precision=lax.Precision.HIGHEST)
            + skip_values[None, :, None] * value_now
        )
        return (updated, (output, updated.astype(jnp.bfloat16)))

    time_major = tuple(
        (
            jnp.moveaxis(member, 1, 0)
            for member in (decays, deltas, inner_values, b_values, c_values)
        )
    )
    last_state, (outputs, states) = lax.scan(advance, start_state, time_major)
    return (jnp.moveaxis(outputs, 0, 1), jnp.moveaxis(states, 0, 1))


def local(
    hidden_states,
    input_gain,
    inner_weight,
    proj_weight,
    step_weight,
    inner_kernel,
    proj_kernel,
    step_bias,
    decay_log,
    skip_gain,
    norm_gain,
    out_weight,
    inner_cache,
    proj_cache,
    state_cache,
    accepted,
    owners,
    tenant_ranges,
):
    layer_count = inner_weight.shape[0]
    row_width = inner_weight.shape[1]
    inner_local = inner_weight.shape[3]
    heads_local = step_weight.shape[2]
    head_size = inner_local // heads_local
    state_size = proj_weight.shape[2] // 2
    requests_local = state_cache.shape[1]
    draft_steps = S
    row_count = lax.axis_size("row")
    col_count = lax.axis_size("col")
    model_width = row_width * row_count
    inner_width = inner_local * col_count
    token_rows = requests_local * draft_steps
    local_ids = jnp.arange(requests_local, dtype=jnp.int32)
    request_ids = lax.axis_index("row") * requests_local + local_ids
    live_mask = jnp.any(
        (request_ids[:, None] >= tenant_ranges[None, :, 0])
        & (request_ids[:, None] < tenant_ranges[None, :, 1]),
        axis=1,
    )
    earlier = (owners[:, None] == owners[None, :]) & (local_ids[None, :] < local_ids[:, None])
    slot_ranks = jnp.sum(earlier.astype(jnp.int32), axis=1)
    slot_ids = owners * SEND_CAP + slot_ranks
    slot_grid = jnp.arange(col_count * SEND_CAP, dtype=jnp.int32)
    step_grid = jnp.arange(draft_steps, dtype=jnp.int32)
    picker = (
        (slot_grid[:, None, None] == slot_ids[None, :, None])
        & (step_grid[None, None, :] == accepted[None, :, None] - 1)
        & live_mask[None, :, None]
    )
    picker = picker.astype(jnp.bfloat16).reshape(col_count * SEND_CAP, token_rows)
    hidden = hidden_states
    step_outputs = []
    chosen_layers = []
    for layer_index in range(layer_count):
        all_tokens = lax.all_gather(hidden, "col", axis=0, tiled=True)
        tokens_f = all_tokens.astype(jnp.float32)
        scaled = (tokens_f * input_gain[layer_index]).astype(jnp.bfloat16)
        square_part = jnp.sum(tokens_f * tokens_f, axis=1)
        inner_part = jnp.dot(
            scaled,
            inner_weight[layer_index].reshape(row_width, 2 * inner_local),
            preferred_element_type=jnp.float32,
        )
        step_part = jnp.dot(scaled, step_weight[layer_index], preferred_element_type=jnp.float32)
        proj_part = jnp.dot(scaled, proj_weight[layer_index], preferred_element_type=jnp.float32)
        inner_sum, step_sum, proj_sum, square_sum = (
            lax.psum_scatter(inner_part, "row", scatter_dimension=0, tiled=True),
            lax.psum_scatter(step_part, "row", scatter_dimension=0, tiled=True),
            lax.psum_scatter(proj_part, "row", scatter_dimension=0, tiled=True),
            lax.psum_scatter(square_part, "row", scatter_dimension=0, tiled=True),
        )
        inverse_rms = lax.rsqrt(square_sum / model_width + EPSILON)
        inner_vals = inner_sum * inverse_rms[:, None]
        gate_vals = inner_vals[:, :inner_local]
        raw_inner = inner_vals[:, inner_local:].reshape(requests_local, draft_steps, inner_local)
        raw_proj = (proj_sum * inverse_rms[:, None]).reshape(
            requests_local, draft_steps, 2 * state_size
        )
        conv_inner = conv_silu(
            inner_cache[layer_index].astype(jnp.float32), raw_inner, inner_kernel[layer_index]
        )
        conv_proj = conv_silu(
            proj_cache[layer_index].astype(jnp.float32), raw_proj, proj_kernel[layer_index]
        )
        deltas = jax.nn.softplus(
            (step_sum * inverse_rms[:, None]).reshape(requests_local, draft_steps, heads_local)
            + step_bias[layer_index]
        )
        decays = jnp.exp(-deltas * jnp.exp(decay_log[layer_index]))
        outputs, states = ssm_scan(
            decays,
            deltas,
            conv_inner.reshape(requests_local, draft_steps, heads_local, head_size),
            conv_proj[..., :state_size],
            conv_proj[..., state_size:],
            skip_gain[layer_index],
            state_cache[layer_index],
        )
        step_outputs.append(states)
        gated_raw = outputs.reshape(token_rows, inner_local) * jax.nn.silu(gate_vals)
        gate_square = lax.psum(jnp.sum(gated_raw * gated_raw, axis=1), "col")
        gated = (
            gated_raw
            * norm_gain[layer_index]
            * lax.rsqrt(gate_square / inner_width + EPSILON)[:, None]
        ).astype(jnp.bfloat16)
        layer_weight = out_weight[layer_index]
        partial_out = jnp.dot(
            lax.all_gather(gated, "row", axis=0, tiled=True),
            layer_weight,
            preferred_element_type=jnp.float32,
        )
        out_sum = lax.psum_scatter(
            partial_out.astype(jnp.bfloat16), "col", scatter_dimension=0, tiled=True
        ).astype(jnp.float32)
        hidden = (hidden.astype(jnp.float32) + out_sum).astype(jnp.bfloat16)
        chosen = jnp.dot(
            picker,
            states.reshape(token_rows, heads_local * head_size * state_size),
            preferred_element_type=jnp.float32,
        )
        chosen = chosen.astype(jnp.bfloat16).reshape(
            col_count, SEND_CAP, heads_local, head_size, state_size
        )
        chosen_layers.append(chosen)
    gathered = lax.all_to_all(
        jnp.stack(chosen_layers, axis=2), "col", split_axis=0, concat_axis=3, tiled=True
    )
    owned_block = gathered[None]
    step_all = jnp.stack(step_outputs, axis=0)
    return (hidden, step_all, owned_block)


def solution(mesh):
    placed = (
        P("col", "row"),
        P(None, "row"),
        P(None, "row", None, "col"),
        P(None, "row", None),
        P(None, "row", "col"),
        P(None, None, "col"),
        P(),
        P(None, "col"),
        P(None, "col"),
        P(None, "col"),
        P(None, "col"),
        P(None, "col", "row"),
        P(None, "row", None, "col"),
        P(None, "row", None, None),
        P(None, "row", "col", None, None),
        P("row"),
        P("row"),
        P(),
    )
    return jax.shard_map(
        local,
        mesh=mesh,
        in_specs=placed,
        out_specs=(
            P("col", "row"),
            P(None, "row", None, "col", None, None),
            P("row", "col", None, None, None, None, None),
        ),
        check_vma=False,
    )
```

profile of v0, /device:TPU:0, one launch (start us, length us, event | category | flops | bytes accessed | tf_op | source)
XLA Modules:
  0.0 788.9 jit_solution(10721165272953729870)
XLA Ops:
  8.6 25.4 %all_gather.12 = bf16[1024,256]{1,0:T(8,128)(2,1)S(1)} all-gather(bf16[64,256]{1,0:T(8,128)(2,1)} %param.22), channel_id=1, replica_groups=mesh['row'=8,'col'=16] {'col'}, dimensions={0}, use_global_device_ids=true | all-gather | bytes 557056 | tf_op jit(solution)/shard_map/all_gather | solution.py:99
  42.9 12.5 %all-reduce = f32[1024]{0:T(1024)S(1)} all-reduce(f32[1024]{0:T(1024)S(1)} %fusion.5), channel_id=3, replica_groups=mesh['row'=8,'col'=16] {'row'}, use_global_device_ids=true, to_apply=%region_2.0.clone | all-reduce | flops 1024 | bytes 8192
  60.8 5.6 reduce-scatter.25.cloned.1.call-done
  69.0 31.3 %reduce-scatter.15.cloned.1.call-done = f32[128,256]{1,0:T(8,128)} async-done(((f32[1024,256]{1,0:T(8,128)}), f32[128,256]{1,0:T(8,128)}) %reduce-scatter.15.cloned.1.call-update) | async-done | bytes 131088 | tf_op jit(solution)/shard_map/reduce_scatter | solution.py:113
  102.1 33.8 %reduce-scatter.13.cloned.1.call-done = f32[128,512]{1,0:T(8,128)} async-done(((f32[1024,512]{1,0:T(8,128)}), f32[128,512]{1,0:T(8,128)}) %reduce-scatter.13.cloned.1.call-update) | async-done | bytes 262160 | tf_op jit(solution)/shard_map/reduce_scatter | solution.py:111
  137.4 5.4 broadcast.153.clone2
  142.7 103.3 %while.28 = (s32[]{:T(128)}, f32[8,4,64,128]{3,2,1,0:T(8,128)S(1)}, f32[16,8,4,64]{3,2,1,0:T(4,128)S(1)}, bf16[16,8,4,64,128]{4,3,2,0,1:T(8,128)(2,1)}, f32[16,8...) while((s32[]{:T(128)}, f32[8,4,64,128]{3,2,1,0:T(8,128)S(1)}, ...), condition=%wide.region_6.0_spmd, body=%wide.region_5.0_spmd.sunk | while | flops 4200450 | bytes 3777949 | solution.py:40
  145.9 2.5 fusion.99
  158.8 2.5 fusion.99
  165.3 2.5 fusion.99
  171.7 2.5 fusion.99
  178.2 2.5 fusion.99
  184.6 2.5 fusion.99
  246.5 40.5 %psum.14 = f32[128]{0:T(128)S(1)} all-reduce(f32[128]{0:T(128)S(1)} %get-tuple-element.179), channel_id=1, replica_groups=mesh['row'=8,'col'=16] {'col'}, use_global_device_ids=true, to_apply=%region_8.9 | all-reduce | flops 128 | bytes 1024 | tf_op jit(solution)/shard_map/psum | solution.py:145
  287.8 13.1 %all_gather.13 = bf16[1024,256]{1,0:T(8,128)(2,1)S(1)} all-gather(bf16[128,256]{1,0:T(8,128)(2,1)S(1)} %multiply_convert_fusion.1), channel_id=1, replica_groups=mesh['row'=8,'col'=16] {'row'}, dimensions={0}, use_global_device_ids=true | all-gather | bytes 589824 | tf_op jit(solution)/shard_map/all_gather | solution.py:153
  302.9 67.3 %reduce-scatter.17.cloned.1.call-done = bf16[64,256]{1,0:T(8,128)(2,1)} async-done(((bf16[1024,256]{1,0:T(8,128)(2,1)}), bf16[64,256]{1,0:T(8,128)(2,1)}) %reduce-scatter.17.cloned.1.call-update) | async-done | bytes 32784 | tf_op jit(solution)/shard_map/reduce_scatter | solution.py:157
  371.0 23.3 %all_gather.14 = bf16[1024,256]{1,0:T(8,128)(2,1)S(1)} all-gather(bf16[64,256]{1,0:T(8,128)(2,1)S(1)} %add_convert_fusion.1), channel_id=1, replica_groups=mesh['row'=8,'col'=16] {'col'}, dimensions={0}, use_global_device_ids=true | all-gather | bytes 557056 | tf_op jit(solution)/shard_map/all_gather | solution.py:99
  400.6 13.3 %reshape.291 = bf16[128,32768]{1,0:T(8,128)(2,1)} reshape(bf16[8,16,4,64,128]{4,3,2,1,0:T(8,128)(2,1)} %bitcast.249) | data formatting | bytes 16777216 | tf_op jit(solution)/shard_map/reshape | solution.py:163
  414.0 4.7 fusion.2
  420.7 12.6 %all-reduce.1 = f32[1024]{0:T(1024)S(1)} all-reduce(f32[1024]{0:T(1024)S(1)} %fusion.7), channel_id=8, replica_groups=mesh['row'=8,'col'=16] {'row'}, use_global_device_ids=true, to_apply=%region_12.13.clone | all-reduce | flops 1024 | bytes 8192
  434.7 24.2 %reduce-scatter.21.cloned.1.call-done = f32[128,256]{1,0:T(8,128)} async-done(((f32[1024,256]{1,0:T(8,128)}), f32[128,256]{1,0:T(8,128)}) %reduce-scatter.21.cloned.1.call-update) | async-done | bytes 131088 | tf_op jit(solution)/shard_map/reduce_scatter | solution.py:113
  460.1 34.4 %reduce-scatter.19.cloned.1.call-done = f32[128,512]{1,0:T(8,128)} async-done(((f32[1024,512]{1,0:T(8,128)}), f32[128,512]{1,0:T(8,128)}) %reduce-scatter.19.cloned.1.call-update) | async-done | bytes 262160 | tf_op jit(solution)/shard_map/reduce_scatter | solution.py:111
  496.0 5.4 broadcast.153.clone
  501.4 70.9 %while.29 = (s32[]{:T(128)}, f32[8,4,64,128]{3,2,1,0:T(8,128)S(1)}, f32[16,8,4,64]{3,2,1,0:T(4,128)S(1)}, bf16[16,8,4,64,128]{4,3,2,0,1:T(8,128)(2,1)}, f32[16,8...) while((s32[]{:T(128)}, f32[8,4,64,128]{3,2,1,0:T(8,128)S(1)}, ...), condition=%wide.region_16.17_spmd, body=%wide.region_15.16_spmd.sunk | while | flops 4200450 | bytes 3778445 | solution.py:40
  572.4 13.3 %reshape.292 = bf16[128,32768]{1,0:T(8,128)(2,1)} reshape(bf16[8,16,4,64,128]{4,3,2,1,0:T(8,128)(2,1)} %bitcast.247) | data formatting | bytes 16777216 | tf_op jit(solution)/shard_map/reshape | solution.py:163
  585.6 4.8 fusion.3
  593.3 7.0 all-to-all-start
  600.8 81.9 %psum.15 = f32[128]{0:T(128)S(1)} all-reduce(f32[128]{0:T(128)S(1)} %get-tuple-element.177), channel_id=1, replica_groups=mesh['row'=8,'col'=16] {'col'}, use_global_device_ids=true, to_apply=%region_18.19 | all-reduce | flops 128 | bytes 1024 | tf_op jit(solution)/shard_map/psum | solution.py:145
  682.8 21.8 %all_gather.15 = bf16[1024,256]{1,0:T(8,128)(2,1)S(1)} all-gather(bf16[128,256]{1,0:T(8,128)(2,1)S(1)} %multiply_convert_fusion), channel_id=1, replica_groups=mesh['row'=8,'col'=16] {'row'}, dimensions={0}, use_global_device_ids=true | all-gather | bytes 589824 | tf_op jit(solution)/shard_map/all_gather | solution.py:153
  705.7 13.8 %pad_maximum_fusion = bf16[2,8,16,4,64,128]{5,4,3,2,1,0:T(8,128)(2,1)} fusion(bf16[1,8,16,4,64,128]{5,4,3,2,1,0:T(8,128)(2,1)} %bitcast.248, bf16[1,8,16,4,64,128]{5,4,3,2,1,0:T(8,128)(2,1)} %bitcast.250), kind=kLoop, calls=%fused_computation.22 | loop fusion | flops 8388608 | bytes 33554432 | tf_op jit(solution)/shard_map/stack | solution.py:174
  719.5 55.1 %reduce-scatter.23.cloned.1.call-done = bf16[64,256]{1,0:T(8,128)(2,1)} async-done(((bf16[1024,256]{1,0:T(8,128)(2,1)}), bf16[64,256]{1,0:T(8,128)(2,1)}) %reduce-scatter.23.cloned.1.call-update) | async-done | bytes 32784 | tf_op jit(solution)/shard_map/reduce_scatter | solution.py:157
  776.1 6.0 copy.143
  (439 shorter events, 201.0 us)
Async XLA Ops:
  7.2 48.3 %copy-start.22 = (f32[2,4]{1,0:T(2,128)S(1)}, f32[2,4]{1,0:T(2,128)}, u32[]{:S(2)}) copy-start(f32[2,4]{1,0:T(2,128)} %param.31) | copy-start | bytes 100
  7.2 48.9 %copy-start.21 = (f32[2,256]{1,0:T(2,128)S(1)}, f32[2,256]{1,0:T(2,128)}, u32[]{:S(2)}) copy-start(f32[2,256]{1,0:T(2,128)} %param.32) | copy-start | bytes 6148
  7.2 49.5 %copy-start.25 = (f32[2,4]{1,0:T(2,128)S(1)}, f32[2,4]{1,0:T(2,128)}, u32[]{:S(2)}) copy-start(f32[2,4]{1,0:T(2,128)} %param.30) | copy-start | bytes 100
  7.2 49.5 %copy-start.24 = (f32[2,4]{1,0:T(2,128)S(1)}, f32[2,4]{1,0:T(2,128)}, u32[]{:S(2)}) copy-start(f32[2,4]{1,0:T(2,128)} %param.29) | copy-start | bytes 100
  7.2 50.0 %copy-start.8 = (f32[2,4,256]{2,1,0:T(4,128)S(1)}, f32[2,4,256]{2,1,0:T(4,128)}, u32[]{:S(2)}) copy-start(f32[2,4,256]{2,1,0:T(4,128)} %param.27) | copy-start | bytes 24580
  7.2 50.6 %copy-start.9 = (f32[2,4,256]{2,1,0:T(4,128)S(1)}, f32[2,4,256]{2,1,0:T(4,128)}, u32[]{:S(2)}) copy-start(f32[2,4,256]{2,1,0:T(4,128)} %param.28) | copy-start | bytes 24580
  7.2 51.2 %copy-start.5 = (bf16[2,8,3,256]{3,1,2,0:T(8,128)(2,1)S(1)}, bf16[2,8,3,256]{3,1,2,0:T(8,128)(2,1)}, u32[]{:S(2)}) copy-start(bf16[2,8,3,256]{3,1,2,0:T(8,128)(2,1)} %param.34) | copy-start | bytes 73732
  7.3 51.2 %copy-start.6 = (bf16[2,8,3,256]{3,1,2,0:T(8,128)(2,1)S(1)}, bf16[2,8,3,256]{3,1,2,0:T(8,128)(2,1)}, u32[]{:S(2)}) copy-start(bf16[2,8,3,256]{3,1,2,0:T(8,128)(2,1)} %param.35) | copy-start | bytes 73732
  7.3 59.2 %reduce-scatter.25.cloned.1.call-start = ((), (), s32[]{:S(2)}) async-start(), calls=%async_computation.15 | async-start | bytes 589824
  35.9 64.4 %reduce-scatter.15.cloned.1.call-start = ((), (), s32[]{:S(2)}) async-start(), calls=%async_computation.10 | async-start | bytes 1179648 | tf_op jit(solution)/shard_map/reduce_scatter | solution.py:113
  38.1 97.8 %reduce-scatter.13.cloned.1.call-start = ((), (), s32[]{:S(2)}) async-start(), calls=%async_computation.9 | async-start | bytes 2359296 | tf_op jit(solution)/shard_map/reduce_scatter | solution.py:111
  41.4 328.8 %reduce-scatter.17.cloned.1.call-start = ((), (), s32[]{:S(2)}) async-start(), calls=%async_computation.11 | async-start | bytes 557056 | tf_op jit(solution)/shard_map/reduce_scatter | solution.py:157
  142.7 227.5 %copy-start.3 = (bf16[64,256]{1,0:T(8,128)(2,1)S(1)}, bf16[64,256]{1,0:T(8,128)(2,1)}, u32[]{:S(2)}) copy-start(bf16[64,256]{1,0:T(8,128)(2,1)} %param.22) | copy-start | bytes 98308
  142.7 253.4 %copy-start.1 = (bf16[2,256,256]{2,1,0:T(8,128)(2,1)S(1)}, bf16[2,256,256]{2,1,0:T(8,128)(2,1)}, u32[]{:S(2)}) copy-start(bf16[2,256,256]{2,1,0:T(8,128)(2,1)} %param.25) | copy-start | bytes 786436
  246.1 152.2 %copy-start.7 = (f32[1,256]{1,0:T(1,128)S(1)}, f32[1,256]{1,0:T(1,128)}, u32[]{:S(2)}) copy-start(f32[1,256]{1,0:T(1,128)} %get-tuple-element.219) | copy-start | bytes 3076
  246.1 154.0 %copy-start.27 = (s32[8]{0:T(128)S(1)}, s32[8]{0:T(128)}, u32[]{:S(2)}) copy-start(s32[8]{0:T(128)} %param.38) | copy-start | bytes 100
  246.1 154.2 %copy-start.23 = (s32[4,2]{0,1:T(2,128)S(1)}, s32[4,2]{0,1:T(2,128)}, u32[]{:S(2)}) copy-start(s32[4,2]{0,1:T(2,128)} %param.39) | copy-start | bytes 100
  246.1 154.3 %copy-start.26 = (s32[8]{0:T(128)S(1)}, s32[8]{0:T(128)}, u32[]{:S(2)}) copy-start(s32[8]{0:T(128)} %param.37) | copy-start | bytes 100
  302.9 130.5 %reduce-scatter.27.cloned.1.call-start = ((), (), s32[]{:S(2)}) async-start(), calls=%async_computation.16 | async-start | bytes 589824
  396.1 62.8 %reduce-scatter.21.cloned.1.call-start = ((), (), s32[]{:S(2)}) async-start(), calls=%async_computation.13 | async-start | bytes 1179648 | tf_op jit(solution)/shard_map/reduce_scatter | solution.py:113
  398.2 96.4 %reduce-scatter.19.cloned.1.call-start = ((), (), s32[]{:S(2)}) async-start(), calls=%async_computation.12 | async-start | bytes 2359296 | tf_op jit(solution)/shard_map/reduce_scatter | solution.py:111
  413.9 46.1 %copy-start.15 = (f32[1,1,256]{2,1,0:T(1,128)S(1)}, f32[1,1,256]{2,1,0:T(1,128)}, u32[]{:S(2)}) copy-start(f32[1,1,256]{2,1,0:T(1,128)} %get-tuple-element.202) | copy-start | bytes 3076
  413.9 46.1 %copy-start.16 = (f32[1,1,256]{2,1,0:T(1,128)S(1)}, f32[1,1,256]{2,1,0:T(1,128)}, u32[]{:S(2)}) copy-start(f32[1,1,256]{2,1,0:T(1,128)} %get-tuple-element.207) | copy-start | bytes 3076
  413.9 46.1 %copy-start.17 = (f32[1,1,256]{2,1,0:T(1,128)S(1)}, f32[1,1,256]{2,1,0:T(1,128)}, u32[]{:S(2)}) copy-start(f32[1,1,256]{2,1,0:T(1,128)} %get-tuple-element.208) | copy-start | bytes 3076
  414.0 81.8 %copy-start.10 = (f32[1,1,256]{2,1,0:T(1,128)S(1)}, f32[1,1,256]{2,1,0:T(1,128)}, u32[]{:S(2)}) copy-start(f32[1,1,256]{2,1,0:T(1,128)} %get-tuple-element.209) | copy-start | bytes 3076
  414.0 81.8 %copy-start.11 = (f32[1,1,256]{2,1,0:T(1,128)S(1)}, f32[1,1,256]{2,1,0:T(1,128)}, u32[]{:S(2)}) copy-start(f32[1,1,256]{2,1,0:T(1,128)} %get-tuple-element.210) | copy-start | bytes 3076
  414.0 81.8 %copy-start.12 = (f32[1,1,256]{2,1,0:T(1,128)S(1)}, f32[1,1,256]{2,1,0:T(1,128)}, u32[]{:S(2)}) copy-start(f32[1,1,256]{2,1,0:T(1,128)} %get-tuple-element.215) | copy-start | bytes 3076
  414.0 81.8 %copy-start.13 = (f32[1,1,256]{2,1,0:T(1,128)S(1)}, f32[1,1,256]{2,1,0:T(1,128)}, u32[]{:S(2)}) copy-start(f32[1,1,256]{2,1,0:T(1,128)} %get-tuple-element.216) | copy-start | bytes 3076
  590.9 91.8 %copy-start.18 = (f32[1,256]{1,0:T(1,128)S(1)}, f32[1,256]{1,0:T(1,128)}, u32[]{:S(2)}) copy-start(f32[1,256]{1,0:T(1,128)} %get-tuple-element.217) | copy-start | bytes 3076
  590.9 113.7 %copy-start.2 = (bf16[2,256,256]{2,1,0:T(8,128)(2,1)S(1)}, bf16[2,256,256]{2,1,0:T(8,128)(2,1)}, u32[]{:S(2)}) copy-start(bf16[2,256,256]{2,1,0:T(8,128)(2,1)} %param.33) | copy-start | bytes 786436
  593.3 182.7 %all-to-all-start = ((bf16[16,2,2,4,64,128]{5,4,3,1,2,0:T(8,128)(2,1)}), bf16[16,2,2,4,64,128]{5,4,3,1,2,0:T(8,128)(2,1)}, u32[]{:S(2)}, u32[]{:S(2)}) async-start(bf16[16,2,2,4,64,128]{5,4,3,1,2,0:T(8,128)(2,1)} %pad_maximum_fusion.1), calls=%async_computation.6 | async-start | bytes 8388608 | tf_op jit(solution)/shard_map/all_to_all | solution.py:170
  600.3 174.4 %reduce-scatter.23.cloned.1.call-start = ((), (), s32[]{:S(2)}) async-start(), calls=%async_computation.14 | async-start | bytes 557056 | tf_op jit(solution)/shard_map/reduce_scatter | solution.py:157
  (6 other events, 172.7 us)
Sparse Core Ops, SparseCore 0:
  36.0 30.4 reduce-scatter.24
  69.5 30.7 reduce-scatter.14
  103.4 32.4 reduce-scatter.12
  303.0 67.1 reduce-scatter.16
  396.2 29.5 reduce-scatter.26
  428.2 30.6 reduce-scatter.20
  462.0 32.5 reduce-scatter.18
  705.8 68.7 reduce-scatter.22
where the time goes:
time: 792 us; the launch traced here: 789 us
  waiting for transfers between devices  252 us (32%)
  blocking collectives  231 us (29%)
  matrix products  105 us (13%)
  other arithmetic  90.8 us (11%)
  local copies, waits for them, and re-layouts  86.9 us (11%)
  between operations  15.4 us (2%)
    psum x2, blocking collectives, local(): gate_square = lax.psum(jnp.sum(gated_raw * gated_raw, axis=1), 'col')  122 us
    reduce_scatter x2, waiting for transfers between devices, local(): lax.psum_scatter(partial_out.astype(jnp.bfloat16), 'col', scatter_dimensi...  122 us
    dot_general x32, matrix products, advance(): jnp.einsum('rhpn,rn->rhp', updated, c_now, precision=lax.Precision.HIGHEST)  80.9 us
    reduce_scatter x2, waiting for transfers between devices, local(): lax.psum_scatter(inner_part, 'row', scatter_dimension=0, tiled=True)  68.3 us
    dynamic_update_slice x64, other arithmetic, ssm_scan(): last_state, (outputs, states) = lax.scan(advance, start_state, time_major)  62.7 us
    reduce_scatter x2, waiting for transfers between devices, local(): lax.psum_scatter(proj_part, 'row', scatter_dimension=0, tiled=True)  55.6 us
    all_gather x2, blocking collectives, local(): all_tokens = lax.all_gather(hidden, 'col', axis=0, tiled=True)  48.8 us
    all_gather x2, blocking collectives, local(): lax.all_gather(gated, 'row', axis=0, tiled=True)  34.9 us
  transfers between devices with their start and end apart: 9, of which 7 were waited for; matrix products, arithmetic and copies ran while one was open for 8% of the time, Pallas kernels for 0%

commit v1 on v0

--- a/solution.py
+++ b/solution.py
@@ -96,7 +96,9 @@
     step_outputs = []
     chosen_layers = []
     for layer_index in range(layer_count):
-        all_tokens = lax.all_gather(hidden, "col", axis=0, tiled=True)
+        all_tokens = jnp.concatenate(
+            lax.all_to_all(jnp.stack([hidden] * lax.axis_size("col")), "col", 0, 0), axis=0
+        )
         tokens_f = all_tokens.astype(jnp.float32)
         scaled = (tokens_f * input_gain[layer_index]).astype(jnp.bfloat16)
         square_part = jnp.sum(tokens_f * tokens_f, axis=1)

time: 792 us -> 833 us (1.052)
  local copies, waits for them, and re-layouts: 86.9 us -> 123 us
  blocking collectives: 231 us -> 198 us
  other arithmetic: 90.8 us -> 114 us
    all_gather x2 -> x0, blocking collectives: 48.8 us -> none  [local(): all_tokens = lax.all_gather(hidden, 'col', axis=0, tiled=True)]
    all_to_all x0 -> x1, blocking collectives: none -> 14.8 us  [local(): lax.all_to_all(jnp.stack([hidden] * lax.axis_size('col')), 'col', 0, 0)]
    mul x32, other arithmetic: 2.37 us -> 13.8 us  [advance(): delta_now[:, :, None] * value_now]
    dynamic_slice x32, local copies, waits for them, and re-layouts: 0.05 us -> 11 us  [ssm_scan(): last_state, (outputs, states) = lax.scan(advance, start_state, time_major)]
    mul x64, local copies, waits for them, and re-layouts: 13.8 us -> 24.7 us  [advance(): delta_now[:, :, None] * value_now]
    mul x32, local copies, waits for them, and re-layouts: 11.3 us -> 22 us  [advance(): (delta_now[:, :, None] * value_now)[:, :, :, None] * b_now[:, None, None, :]]
    all_to_all x0 -> x1, waiting for transfers between devices: none -> 10.7 us  [local(): lax.all_to_all(jnp.stack([hidden] * lax.axis_size('col')), 'col', 0, 0)]
    dynamic_update_slice x64, other arithmetic: 62.7 us -> 73.2 us  [ssm_scan(): last_state, (outputs, states) = lax.scan(advance, start_state, time_major)]
  transfers between devices with their start and end apart: 9 -> 10, of which waited for: 7 -> 8; matrix products, arithmetic and copies ran while one was open for 8% -> 7% of each run, Pallas kernels for 0% -> 0%
where the time goes in v1:
time: 833 us; the launch traced here: 826 us
  waiting for transfers between devices  258 us (31%)
  blocking collectives  198 us (24%)
  local copies, waits for them, and re-layouts  123 us (15%)
  other arithmetic  114 us (14%)
  matrix products  103 us (12%)
  between operations  15.4 us (2%)
  starting transfers between devices  15.3 us (2%)
    psum x2, blocking collectives, local(): gate_square = lax.psum(jnp.sum(gated_raw * gated_raw, axis=1), 'col')  123 us
    reduce_scatter x2, waiting for transfers between devices, local(): lax.psum_scatter(partial_out.astype(jnp.bfloat16), 'col', scatter_dimensi...  122 us
    dot_general x32, matrix products, advance(): jnp.einsum('rhpn,rn->rhp', updated, c_now, precision=lax.Precision.HIGHEST)  80.9 us
    dynamic_update_slice x64, other arithmetic, ssm_scan(): last_state, (outputs, states) = lax.scan(advance, start_state, time_major)  73.2 us
    reduce_scatter x2, waiting for transfers between devices, local(): lax.psum_scatter(inner_part, 'row', scatter_dimension=0, tiled=True)  67.7 us
    reduce_scatter x2, waiting for transfers between devices, local(): lax.psum_scatter(proj_part, 'row', scatter_dimension=0, tiled=True)  54.4 us
    all_gather x2, blocking collectives, local(): lax.all_gather(gated, 'row', axis=0, tiled=True)  34.7 us
    reshape x2, local copies, waits for them, and re-layouts, local(): states.reshape(token_rows, heads_local * head_size * state_size)  26.6 us
  transfers between devices with their start and end apart: 10, of which 8 were waited for; matrix products, arithmetic and copies ran while one was open for 7% of the time, Pallas kernels for 0%

profile of v1, /device:TPU:0, one launch (start us, length us, event | category | flops | bytes accessed | tf_op | source)
XLA Modules:
  0.0 826.3 jit_solution(9932181819673859142)
XLA Ops:
  8.9 8.0 all-to-all-start
  17.7 10.7 %all-to-all-done = bf16[16,64,256]{2,1,0:T(8,128)(2,1)S(1)} async-done(((bf16[16,64,256]{2,1,0:T(8,128)(2,1)}), bf16[16,64,256]{2,1,0:T(8,128)(2,1)S(1)}, u32[]{:S(2)}, u32[]{:S(2)}) %all-to-all-start) | async-done | bytes 524320 | tf_op jit(solution)/shard_map/all_to_all | solution.py:100
  43.2 13.5 %all-reduce = f32[1024]{0:T(1024)S(1)} all-reduce(f32[1024]{0:T(1024)S(1)} %reduce_sum.50), channel_id=3, replica_groups=mesh['row'=8,'col'=16] {'row'}, use_global_device_ids=true, to_apply=%region_2.0.clone | all-reduce | flops 1024 | bytes 8192
  61.6 31.2 %reduce-scatter.15.cloned.1.call-done = f32[128,256]{1,0:T(8,128)} async-done(((f32[1024,256]{1,0:T(8,128)}), f32[128,256]{1,0:T(8,128)}) %reduce-scatter.15.cloned.1.call-update) | async-done | bytes 131088 | tf_op jit(solution)/shard_map/reduce_scatter | solution.py:115
  94.6 33.9 %reduce-scatter.13.cloned.1.call-done = f32[128,512]{1,0:T(8,128)} async-done(((f32[1024,512]{1,0:T(8,128)}), f32[128,512]{1,0:T(8,128)}) %reduce-scatter.13.cloned.1.call-update) | async-done | bytes 262160 | tf_op jit(solution)/shard_map/reduce_scatter | solution.py:113
  130.0 5.4 broadcast.181.clone2
  135.3 92.8 %while.28 = (s32[]{:T(128)}, f32[8,4,64,128]{3,2,1,0:T(8,128)S(1)}, f32[16,8,4,64]{3,2,1,0:T(4,128)S(1)}, bf16[16,8,4,64,128]{4,3,2,0,1:T(8,128)(2,1)}, f32[16,8...) while((s32[]{:T(128)}, f32[8,4,64,128]{3,2,1,0:T(8,128)S(1)}, ...), condition=%wide.region_6.0_spmd, body=%wide.region_5.0_spmd.sunk | while | flops 4200450 | bytes 3778445 | solution.py:40
  150.1 2.5 fusion.99
  161.7 2.5 fusion.99
  167.5 2.5 fusion.99
  173.3 2.5 fusion.99
  185.0 2.5 fusion.99
  190.7 2.5 fusion.99
  228.5 40.6 %psum.14 = f32[128]{0:T(128)S(1)} all-reduce(f32[128]{0:T(128)S(1)} %get-tuple-element.179), channel_id=1, replica_groups=mesh['row'=8,'col'=16] {'col'}, use_global_device_ids=true, to_apply=%region_8.9 | all-reduce | flops 128 | bytes 1024 | tf_op jit(solution)/shard_map/psum | solution.py:147
  269.2 13.1 %all_gather.6 = bf16[1024,256]{1,0:T(8,128)(2,1)S(1)} all-gather(bf16[128,256]{1,0:T(8,128)(2,1)S(1)} %multiply_convert_fusion.1), channel_id=1, replica_groups=mesh['row'=8,'col'=16] {'row'}, dimensions={0}, use_global_device_ids=true | all-gather | bytes 589824 | tf_op jit(solution)/shard_map/all_gather | solution.py:155
  283.5 67.3 %reduce-scatter.17.cloned.1.call-done = bf16[64,256]{1,0:T(8,128)(2,1)} async-done(((bf16[1024,256]{1,0:T(8,128)(2,1)}), bf16[64,256]{1,0:T(8,128)(2,1)}) %reduce-scatter.17.cloned.1.call-update) | async-done | bytes 32784 | tf_op jit(solution)/shard_map/reduce_scatter | solution.py:159
  351.7 14.8 %all_to_all.25 = bf16[16,64,256]{2,1,0:T(8,128)(2,1)S(1)} all-to-all(bf16[16,64,256]{2,1,0:T(8,128)(2,1)S(1)} %stack.13), channel_id=1, replica_groups=mesh['row'=8,'col'=16] {'col'}, dimensions={0} | all-to-all | bytes 1048576 | tf_op jit(solution)/shard_map/all_to_all | solution.py:100
  372.7 13.3 %reshape.335 = bf16[128,32768]{1,0:T(8,128)(2,1)} reshape(bf16[8,16,4,64,128]{4,3,2,1,0:T(8,128)(2,1)} %bitcast.257) | data formatting | bytes 16777216 | tf_op jit(solution)/shard_map/reshape | solution.py:165
  386.0 4.7 fusion.2
  391.2 12.6 %all-reduce.1 = f32[1024]{0:T(1024)S(1)} all-reduce(f32[1024]{0:T(1024)S(1)} %reduce_sum.53), channel_id=8, replica_groups=mesh['row'=8,'col'=16] {'row'}, use_global_device_ids=true, to_apply=%region_12.13.clone | all-reduce | flops 1024 | bytes 8192
  406.4 23.2 %reduce-scatter.21.cloned.1.call-done = f32[128,256]{1,0:T(8,128)} async-done(((f32[1024,256]{1,0:T(8,128)}), f32[128,256]{1,0:T(8,128)}) %reduce-scatter.21.cloned.1.call-update) | async-done | bytes 131088 | tf_op jit(solution)/shard_map/reduce_scatter | solution.py:115
  431.4 33.8 %reduce-scatter.19.cloned.1.call-done = f32[128,512]{1,0:T(8,128)} async-done(((f32[1024,512]{1,0:T(8,128)}), f32[128,512]{1,0:T(8,128)}) %reduce-scatter.19.cloned.1.call-update) | async-done | bytes 262160 | tf_op jit(solution)/shard_map/reduce_scatter | solution.py:113
  468.9 5.4 broadcast.181.clone
  474.3 135.8 %while.29 = (s32[]{:T(128)}, f32[8,4,64,128]{3,2,1,0:T(8,128)S(1)}, f32[16,8,4,64]{3,2,1,0:T(4,128)}, bf16[16,8,4,64,128]{4,3,2,0,1:T(8,128)(2,1)}, f32[16,8,4]{...) while((s32[]{:T(128)}, f32[8,4,64,128]{3,2,1,0:T(8,128)S(1)}, ...), condition=%wide.region_16.17_spmd, body=%wide.region_15.16_spmd.sunk | while | flops 4200450 | bytes 3769757 | solution.py:40
  610.1 13.3 %reshape.336 = bf16[128,32768]{1,0:T(8,128)(2,1)} reshape(bf16[8,16,4,64,128]{4,3,2,1,0:T(8,128)(2,1)} %bitcast.255) | data formatting | bytes 16777216 | tf_op jit(solution)/shard_map/reshape | solution.py:165
  623.4 4.6 fusion.3
  630.9 7.0 all-to-all-start.2
  638.4 81.9 %psum.15 = f32[128]{0:T(128)S(1)} all-reduce(f32[128]{0:T(128)S(1)} %get-tuple-element.177), channel_id=1, replica_groups=mesh['row'=8,'col'=16] {'col'}, use_global_device_ids=true, to_apply=%region_18.19 | all-reduce | flops 128 | bytes 1024 | tf_op jit(solution)/shard_map/psum | solution.py:147
  720.5 21.6 %all_gather.7 = bf16[1024,256]{1,0:T(8,128)(2,1)S(1)} all-gather(bf16[128,256]{1,0:T(8,128)(2,1)S(1)} %multiply_convert_fusion), channel_id=1, replica_groups=mesh['row'=8,'col'=16] {'row'}, dimensions={0}, use_global_device_ids=true | all-gather | bytes 589824 | tf_op jit(solution)/shard_map/all_gather | solution.py:155
  743.2 13.8 %pad_maximum_fusion = bf16[2,8,16,4,64,128]{5,4,3,2,1,0:T(8,128)(2,1)} fusion(bf16[1,8,16,4,64,128]{5,4,3,2,1,0:T(8,128)(2,1)} %bitcast.256, bf16[1,8,16,4,64,128]{5,4,3,2,1,0:T(8,128)(2,1)} %bitcast.258), kind=kLoop, calls=%fused_computation.22 | loop fusion | flops 8388608 | bytes 33554432 | tf_op jit(solution)/shard_map/stack | solution.py:176
  757.1 55.1 %reduce-scatter.23.cloned.1.call-done = bf16[64,256]{1,0:T(8,128)(2,1)} async-done(((bf16[1024,256]{1,0:T(8,128)(2,1)}), bf16[64,256]{1,0:T(8,128)(2,1)}) %reduce-scatter.23.cloned.1.call-update) | async-done | bytes 32784 | tf_op jit(solution)/shard_map/reduce_scatter | solution.py:159
  813.5 6.0 copy.143
  (440 shorter events, 260.6 us)
Async XLA Ops:
  7.2 28.8 %copy-start.26 = (u32[128]{0:T(128)S(1)}, u32[128]{0:T(128)}, u32[]{:S(2)}) copy-start(u32[128]{0:T(128)} %constant.80) | copy-start | bytes 1540
  7.2 30.0 %copy-start.20 = (f32[2,4]{1,0:T(2,128)S(1)}, f32[2,4]{1,0:T(2,128)}, u32[]{:S(2)}) copy-start(f32[2,4]{1,0:T(2,128)} %param.31) | copy-start | bytes 100
  7.2 30.6 %copy-start.19 = (f32[2,256]{1,0:T(2,128)S(1)}, f32[2,256]{1,0:T(2,128)}, u32[]{:S(2)}) copy-start(f32[2,256]{1,0:T(2,128)} %param.32) | copy-start | bytes 6148
  7.2 31.1 %copy-start.23 = (f32[2,4]{1,0:T(2,128)S(1)}, f32[2,4]{1,0:T(2,128)}, u32[]{:S(2)}) copy-start(f32[2,4]{1,0:T(2,128)} %param.30) | copy-start | bytes 100
  7.2 31.1 %copy-start.22 = (f32[2,4]{1,0:T(2,128)S(1)}, f32[2,4]{1,0:T(2,128)}, u32[]{:S(2)}) copy-start(f32[2,4]{1,0:T(2,128)} %param.29) | copy-start | bytes 100
  7.2 31.7 %copy-start.10 = (f32[2,4,256]{2,1,0:T(4,128)S(1)}, f32[2,4,256]{2,1,0:T(4,128)}, u32[]{:S(2)}) copy-start(f32[2,4,256]{2,1,0:T(4,128)} %param.27) | copy-start | bytes 24580
  7.2 32.3 %copy-start.11 = (f32[2,4,256]{2,1,0:T(4,128)S(1)}, f32[2,4,256]{2,1,0:T(4,128)}, u32[]{:S(2)}) copy-start(f32[2,4,256]{2,1,0:T(4,128)} %param.28) | copy-start | bytes 24580
  7.2 32.9 %copy-start.7 = (bf16[2,8,3,256]{3,1,2,0:T(8,128)(2,1)S(1)}, bf16[2,8,3,256]{3,1,2,0:T(8,128)(2,1)}, u32[]{:S(2)}) copy-start(bf16[2,8,3,256]{3,1,2,0:T(8,128)(2,1)} %param.34) | copy-start | bytes 73732
  7.2 33.5 %copy-start.8 = (bf16[2,8,3,256]{3,1,2,0:T(8,128)(2,1)S(1)}, bf16[2,8,3,256]{3,1,2,0:T(8,128)(2,1)}, u32[]{:S(2)}) copy-start(bf16[2,8,3,256]{3,1,2,0:T(8,128)(2,1)} %param.35) | copy-start | bytes 73732
  8.9 19.5 %all-to-all-start = ((bf16[16,64,256]{2,1,0:T(8,128)(2,1)}), bf16[16,64,256]{2,1,0:T(8,128)(2,1)S(1)}, u32[]{:S(2)}, u32[]{:S(2)}) async-start(bf16[16,64,256]{2,1,0:T(8,128)(2,1)} %stack.12), calls=%async_computation | async-start | bytes 1048576 | tf_op jit(solution)/shard_map/all_to_all | solution.py:100
  16.9 42.3 %reduce-scatter.25.cloned.1.call-start = ((), (), s32[]{:S(2)}) async-start(), calls=%async_computation.17 | async-start | bytes 589824
  30.4 62.4 %reduce-scatter.15.cloned.1.call-start = ((), (), s32[]{:S(2)}) async-start(), calls=%async_computation.12 | async-start | bytes 1179648 | tf_op jit(solution)/shard_map/reduce_scatter | solution.py:115
  32.7 95.9 %reduce-scatter.13.cloned.1.call-start = ((), (), s32[]{:S(2)}) async-start(), calls=%async_computation.11 | async-start | bytes 2359296 | tf_op jit(solution)/shard_map/reduce_scatter | solution.py:113
  35.9 314.9 %reduce-scatter.17.cloned.1.call-start = ((), (), s32[]{:S(2)}) async-start(), calls=%async_computation.13 | async-start | bytes 557056 | tf_op jit(solution)/shard_map/reduce_scatter | solution.py:159
  135.3 147.0 %copy-start.3 = (bf16[2,256,256]{2,1,0:T(8,128)(2,1)S(1)}, bf16[2,256,256]{2,1,0:T(8,128)(2,1)}, u32[]{:S(2)}) copy-start(bf16[2,256,256]{2,1,0:T(8,128)(2,1)} %param.33) | copy-start | bytes 786436
  135.3 215.5 %copy-start.5 = (bf16[64,256]{1,0:T(8,128)(2,1)S(1)}, bf16[64,256]{1,0:T(8,128)(2,1)}, u32[]{:S(2)}) copy-start(bf16[64,256]{1,0:T(8,128)(2,1)} %param.22) | copy-start | bytes 98308
  135.3 231.4 %copy-start.12 = (bf16[2,256,4]{1,2,0:T(4,128)(2,1)S(1)}, bf16[2,256,4]{1,2,0:T(4,128)(2,1)}, u32[]{:S(2)}) copy-start(bf16[2,256,4]{1,2,0:T(4,128)(2,1)} %param.26) | copy-start | bytes 12292
  228.1 144.0 %copy-start.25 = (s32[8]{0:T(128)S(1)}, s32[8]{0:T(128)}, u32[]{:S(2)}) copy-start(s32[8]{0:T(128)} %param.38) | copy-start | bytes 100
  228.1 144.2 %copy-start.21 = (s32[4,2]{0,1:T(2,128)S(1)}, s32[4,2]{0,1:T(2,128)}, u32[]{:S(2)}) copy-start(s32[4,2]{0,1:T(2,128)} %param.39) | copy-start | bytes 100
  228.1 144.2 %copy-start.24 = (s32[8]{0:T(128)S(1)}, s32[8]{0:T(128)}, u32[]{:S(2)}) copy-start(s32[8]{0:T(128)} %param.37) | copy-start | bytes 100
  283.5 120.4 %reduce-scatter.27.cloned.1.call-start = ((), (), s32[]{:S(2)}) async-start(), calls=%async_computation.18 | async-start | bytes 589824
  367.9 61.7 %reduce-scatter.21.cloned.1.call-start = ((), (), s32[]{:S(2)}) async-start(), calls=%async_computation.15 | async-start | bytes 1179648 | tf_op jit(solution)/shard_map/reduce_scatter | solution.py:115
  370.2 95.0 %reduce-scatter.19.cloned.1.call-start = ((), (), s32[]{:S(2)}) async-start(), calls=%async_computation.14 | async-start | bytes 2359296 | tf_op jit(solution)/shard_map/reduce_scatter | solution.py:113
  386.0 44.7 %copy-start.6 = (f32[8,3,256]{2,0,1:T(8,128)S(1)}, f32[8,3,256]{2,0,1:T(8,128)}, u32[]{:S(2)}) copy-start(f32[8,3,256]{2,0,1:T(8,128)} %get-tuple-element.197) | copy-start | bytes 73732
  386.0 44.7 %copy-start.13 = (f32[1,1,256]{2,1,0:T(1,128)S(1)}, f32[1,1,256]{2,1,0:T(1,128)}, u32[]{:S(2)}) copy-start(f32[1,1,256]{2,1,0:T(1,128)} %get-tuple-element.206) | copy-start | bytes 3076
  386.0 44.7 %copy-start.14 = (f32[1,1,256]{2,1,0:T(1,128)S(1)}, f32[1,1,256]{2,1,0:T(1,128)}, u32[]{:S(2)}) copy-start(f32[1,1,256]{2,1,0:T(1,128)} %get-tuple-element.211) | copy-start | bytes 3076
  386.0 44.7 %copy-start.15 = (f32[1,1,256]{2,1,0:T(1,128)S(1)}, f32[1,1,256]{2,1,0:T(1,128)}, u32[]{:S(2)}) copy-start(f32[1,1,256]{2,1,0:T(1,128)} %get-tuple-element.212) | copy-start | bytes 3076
  628.5 91.9 %copy-start.16 = (f32[1,256]{1,0:T(1,128)S(1)}, f32[1,256]{1,0:T(1,128)}, u32[]{:S(2)}) copy-start(f32[1,256]{1,0:T(1,128)} %get-tuple-element.221) | copy-start | bytes 3076
  628.5 113.6 %copy-start.4 = (bf16[2,256,256]{2,1,0:T(8,128)(2,1)S(1)}, bf16[2,256,256]{2,1,0:T(8,128)(2,1)}, u32[]{:S(2)}) copy-start(bf16[2,256,256]{2,1,0:T(8,128)(2,1)} %param.33) | copy-start | bytes 786436
  630.9 182.6 %all-to-all-start.2 = ((bf16[16,2,2,4,64,128]{5,4,3,1,2,0:T(8,128)(2,1)}), bf16[16,2,2,4,64,128]{5,4,3,1,2,0:T(8,128)(2,1)}, u32[]{:S(2)}, u32[]{:S(2)}) async-start(bf16[16,2,2,4,64,128]{5,4,3,1,2,0:T(8,128)(2,1)} %pad_maximum_fusion.1), calls=%async_computation.8 | async-start | bytes 8388608 | tf_op jit(solution)/shard_map/all_to_all | solution.py:172
  638.0 174.1 %reduce-scatter.23.cloned.1.call-start = ((), (), s32[]{:S(2)}) async-start(), calls=%async_computation.16 | async-start | bytes 557056 | tf_op jit(solution)/shard_map/reduce_scatter | solution.py:159
  743.2 68.9 %copy-start.2 = (bf16[64,256]{1,0:T(8,128)(2,1)S(1)}, bf16[64,256]{1,0:T(8,128)(2,1)}, u32[]{:S(2)}) copy-start(bf16[64,256]{1,0:T(8,128)(2,1)} %copy-done.1) | copy-start | bytes 98308
  (5 other events, 68.5 us)
Sparse Core Ops, SparseCore 0:
  30.5 28.5 reduce-scatter.24
  62.2 30.5 reduce-scatter.14
  96.0 32.5 reduce-scatter.12
  283.6 67.2 reduce-scatter.16
  368.0 28.3 reduce-scatter.26
  398.8 30.7 reduce-scatter.20
  432.7 32.4 reduce-scatter.18
  743.3 68.7 reduce-scatter.22
